TPU v7x, 32 devices: a whole 2x2x4 slice. The times are simulated.
32 devices in a mesh: dp: 8 (over z, y), mp: 4 (over x, core).
Axes of the slice: x: 2, y: 2, z: 4, core: 2. Of those that a mesh axis runs over, the one named last changes fastest.
Arguments:
- query: bfloat16 [4096, 4096], P('dp', 'mp'), may hold values from -6 to 6
- passage: bfloat16 [4096, 4096], P('dp', 'mp'), may hold values from -6 to 6
- query_scale: bfloat16 [4096], P('dp'), may hold values from 0.4 to 2.5
- passage_scale: bfloat16 [4096], P('dp'), may hold values from 0.4 to 2.5
- partners: int32 [8, 3], P('dp'), may hold values from 0 to 3, as said below
- counts: int32 [8], replicated, may hold values from 256 to 512, as said below
Outputs:
- loss: float32 [], replicated
- grad_query: bfloat16 [4096, 4096], P('dp', 'mp')
- grad_passage: bfloat16 [4096, 4096], P('dp', 'mp')
Inputs may be any that keep to these rules, and one draw needn't show every extreme that they name: `partners`: each nonzero entry of a row is a distinct distance; block 0 and the last 3 blocks use all 3 slots. `counts`: some block has all 512 rows valid.
All inputs are finite; a program needn't handle non-finite values.
Results may differ from a plain program's by a relative error of at most 0.004.
Values may be sent and summed in bfloat16 or wider, within the bound.
A program may use at most 64 MiB of HBM per device.

v0:
```python
import math
import jax
import jax.numpy as jnp
from jax import lax
from jax.sharding import PartitionSpec as P

D = 4096
WIN = 3


def shifted(value, axis, steps):
    count = lax.axis_size(axis)
    pairs = [(source, (source + steps) % count) for source in range(count)]
    return lax.ppermute(value, axis, pairs)


def local(query, passage, query_scale, passage_scale, partners, counts):
    inv = 1.0 / math.sqrt(D)
    rows = query.shape[0]
    mine = lax.axis_index("dp")
    ndev = lax.axis_size("dp")
    block_ids = jnp.arange(counts.shape[0], dtype=jnp.int32)

    def count_of(block):
        return jnp.sum(jnp.where(block_ids == block, counts, 0))

    far_rows = []
    far_scales = []
    far_counts = []
    for offset in range(1, WIN + 1):
        moved_rows, moved_scales = shifted((passage, passage_scale), "dp", -offset)
        far_rows.append(moved_rows)
        far_scales.append(moved_scales)
        far_counts.append(count_of((mine + offset) % ndev))
    offsets = partners[0]
    pick = jnp.clip(offsets - 1, 0, WIN - 1)
    keys = jnp.concatenate([passage[None], jnp.take(jnp.stack(far_rows), pick, axis=0)], axis=0)
    key_scales = jnp.concatenate(
        [passage_scale[None], jnp.take(jnp.stack(far_scales), pick, axis=0)], axis=0
    ).astype(jnp.float32)
    own_count = count_of(mine)
    key_counts = jnp.concatenate([own_count[None], jnp.take(jnp.stack(far_counts), pick)])
    live = jnp.concatenate([jnp.array([True]), offsets > 0])
    raw = jnp.einsum("id,kjd->kij", query, keys, preferred_element_type=jnp.float32)
    column = jnp.arange(rows, dtype=jnp.int32)
    col_ok = live[:, None] & (column[None, :] < key_counts[:, None])
    summed = lax.psum_scatter(raw, "mp", scatter_dimension=1, tiled=True)
    share = summed.shape[1]
    start = lax.axis_index("mp") * share
    row_ids = start + jnp.arange(share, dtype=jnp.int32)
    row_scale = lax.dynamic_slice_in_dim(query_scale, start, share).astype(jnp.float32)
    scores = summed * (row_scale * inv)[None, :, None] * key_scales[:, None, :]
    masked = jnp.where(col_ok[:, None, :], scores, -jnp.inf)
    top = jnp.max(masked, axis=(0, 2))
    weights = jnp.exp(masked - top[None, :, None])
    total = jnp.sum(weights, axis=(0, 2))
    lse = top + jnp.log(total)
    valid = row_ids < own_count
    diagonal = column[None, :] == row_ids[:, None]
    positive = jnp.sum(jnp.where(diagonal, scores[0], 0.0), axis=1)
    loss_rows = jnp.where(valid, lse - positive, 0.0)
    grads = weights / total[None, :, None]
    grads = jnp.concatenate([(grads[0] - diagonal.astype(jnp.float32))[None], grads[1:]], axis=0)
    grads = jnp.where(valid[None, :, None], grads, 0.0)
    key_weight = (grads * key_scales[:, None, :]).astype(jnp.bfloat16)
    row_weight = (grads * row_scale[None, :, None]).astype(jnp.bfloat16)
    loss_sum = jnp.sum(loss_rows)
    valid_sum = jnp.sum(valid.astype(jnp.float32))
    key_weight, row_weight = (
        lax.all_gather(key_weight, "mp", axis=1, tiled=True),
        lax.all_gather(row_weight, "mp", axis=1, tiled=True),
    )
    loss_all, valid_all = lax.psum((loss_sum, valid_sum), ("dp", "mp"))
    grad_query = jnp.einsum(
        "kij,kjd->id", key_weight, keys, preferred_element_type=jnp.float32
    ).astype(jnp.bfloat16)
    collected = jnp.einsum("ij,id->jd", row_weight[0], query, preferred_element_type=jnp.float32)
    far_parts = jnp.einsum(
        "kij,id->kjd", row_weight[1:], query, preferred_element_type=jnp.float32
    ).astype(jnp.bfloat16)
    for offset in range(1, WIN + 1):
        chosen = offsets == offset
        outgoing = jnp.sum(
            jnp.where(chosen[:, None, None], far_parts, jnp.zeros_like(far_parts)), axis=0
        )
        arrived = shifted(outgoing, "dp", offset)
        collected = collected + arrived.astype(jnp.float32)
    loss = loss_all / valid_all
    return (loss, grad_query, collected.astype(jnp.bfloat16))


def solution(mesh):
    return jax.shard_map(
        local,
        mesh=mesh,
        in_specs=(P("dp", "mp"), P("dp", "mp"), P("dp"), P("dp"), P("dp", None), P()),
        out_specs=(P(), P("dp", "mp"), P("dp", "mp")),
        check_vma=False,
    )
```

profile of v0, /device:TPU:0, one launch (start us, length us, event | category | flops | bytes accessed | tf_op | source)
XLA Modules:
  0.0 335.3 jit_solution(15261544324831672226)
XLA Ops:
  7.2 5.1 %collective-permute-start.2 = (bf16[512,1024]{1,0:T(8,128)(2,1)}, bf16[512,1024]{1,0:T(8,128)(2,1)S(1)}, u32[]{:S(2)}, u32[]{:S(2)}) collective-permute-start(bf16[512,1024]{1,0:T(8,128)(2,1)} %param.8), channel_id=1, source_target_pairs={{0,20},{4,24},{8,28},{12,0},{16,4},{20,8},{24,12},{28,16},{1,21},{... | collective-permute-start | bytes 3145736 | tf_op jit(solution)/shard_map/ppermute | solution.py:14
  12.3 1.3 collective-permute-start.1
  14.2 1.4 fusion.12
  15.6 2.1 pad_add_fusion.1
  17.6 0.7 fusion.15
  18.9 0.7 broadcast_select_fusion.2
  19.6 16.6 %collective-permute-done.2 = bf16[512,1024]{1,0:T(8,128)(2,1)S(1)} collective-permute-done((bf16[512,1024]{1,0:T(8,128)(2,1)}, bf16[512,1024]{1,0:T(8,128)(2,1)S(1)}, u32[]{:S(2)}, u32[]{:S(2)}) %collective-permute-start.2) | collective-permute-done | bytes 1048608 | tf_op jit(solution)/shard_map/ppermute | solution.py:14
  36.2 23.7 %collective-permute-done.1 = bf16[512,1024]{1,0:T(8,128)(2,1)S(1)} collective-permute-done((bf16[512,1024]{1,0:T(8,128)(2,1)}, bf16[512,1024]{1,0:T(8,128)(2,1)S(1)}, u32[]{:S(2)}, u32[]{:S(2)}) %collective-permute-start.1) | collective-permute-done | bytes 1048608 | tf_op jit(solution)/shard_map/ppermute | solution.py:14
  59.9 20.1 %collective-permute-done = bf16[512,1024]{1,0:T(8,128)(2,1)} collective-permute-done((bf16[512,1024]{1,0:T(8,128)(2,1)}, bf16[512,1024]{1,0:T(8,128)(2,1)}, u32[]{:S(2)}, u32[]{:S(2)}) %collective-permute-start) | collective-permute-done | bytes 1048608 | tf_op jit(solution)/shard_map/ppermute | solution.py:14
  80.0 3.2 pad_maximum_fusion.1
  83.2 4.4 %gather_fusion.1 = bf16[3,512,1024]{2,1,0:T(8,128)(2,1)} fusion(bf16[3,512,1024]{2,1,0:T(8,128)(2,1)} %pad_maximum_fusion.1, s32[1024]{0:T(1024)S(1)} %pad_clamp_fusion), kind=kCustom, calls=%fused_computation.1 | custom fusion | bytes 6291468 | tf_op jit(solution)/shard_map/jit(_take)/gather | solution.py:37
  87.7 2.3 broadcast_select_fusion
  90.0 1.7 copy-done.1
  91.7 4.3 %fusion.2 = f32[4,512,512]{1,2,0:T(8,128)} fusion(bf16[3,512,1024]{2,1,0:T(8,128)(2,1)S(1)} %broadcast_select_fusion, bf16[1,512,1024]{2,1,0:T(8,128)(2,1)S(1)} %bitcast.50, bf16[512,1024]{1,0:T(8,128)(2,1)S(1)} %copy-done), kind=kOutput, calls=%fused_computation.12 | convolution fusion | flops 2149580800 | bytes 9437184 | tf_op jit(solution)/shard_map/id,kjd->kij/dot_general | solution.py:44
  96.7 3.3 collective-permute-start.5
  100.0 23.8 %collective-permute-start.4 = (bf16[512]{0:T(512)(128)(2,1)S(1)}, bf16[512]{0:T(512)(128)(2,1)S(1)}, u32[]{:S(2)}, u32[]{:S(2)}) collective-permute-start(bf16[512]{0:T(512)(128)(2,1)S(1)} %copy-done.3), channel_id=1, source_target_pairs={{0,24},{4,28},{8,0},{12,4},{16,8},{20,12},{24,16},{28,20},{1,25},{... | collective-permute-start | bytes 3080 | tf_op jit(solution)/shard_map/ppermute | solution.py:14
  124.5 0.7 pad_add_fusion.2
  125.5 0.9 collective-permute-done.4
  126.4 1.0 collective-permute-done.3
  128.1 36.8 %reduce-scatter.2.cloned.1.call-done = f32[4,128,512]{1,2,0:T(8,128)} async-done(((f32[4,512,512]{1,2,0:T(8,128)}), f32[4,128,512]{1,2,0:T(8,128)}) %reduce-scatter.2.cloned.1.call-update) | async-done | bytes 1048592 | tf_op jit(solution)/shard_map/reduce_scatter | solution.py:47
  164.8 1.8 select_reduce_fusion.3
  167.6 1.3 convert_reduce_fusion
  168.9 1.3 multiply_convert_fusion
  170.3 0.7 all-gather.3.cloned.1.call-update
  171.0 22.2 %all-gather.5.cloned.1.call-done = bf16[4,512,512]{1,2,0:T(8,128)(2,1)} async-done(((bf16[4,128,512]{1,2,0:T(8,128)(2,1)}), bf16[4,512,512]{1,2,0:T(8,128)(2,1)}) %all-gather.5.cloned.1.call-update) | async-done | bytes 2097168 | tf_op jit(solution)/shard_map/all_gather | solution.py:71
  193.2 5.5 %select_reduce_fusion.2 = (bf16[512,1024]{1,0:T(8,128)(2,1)S(1)}, bf16[512,1024]{1,0:T(8,128)(2,1)}, bf16[512,1024]{1,0:T(8,128)(2,1)}) fusion(pred[3]{0:T(512)(128)(4,1)S(1)} %get-tuple-element.24, pred[3]{0:T(512)(128)(4,1)S(1)} %get-tuple-element.26, pred[3]{0:T(512)(128)(4,1)S(1)} %get-tuple-element.23, ...), kind=kOutput, calls=%fused_computation.7 | convolution fusion | flops 1620049920 | bytes 6291465 | tf_op jit(solution)/shard_map/kij,id->kjd/dot_general | solution.py:78
  198.6 2.4 collective-permute-start.8
  201.0 1.5 collective-permute-start.7
  202.5 1.5 collective-permute-start.6
  204.0 112.5 %all-reduce = (f32[]{:T(128)}, f32[]{:T(128)}) all-reduce(f32[]{:T(128)} %get-tuple-element.7, f32[]{:T(128)} %get-tuple-element.6), channel_id=1, replica_groups=mesh['dp'=8,'mp'=4] {'dp','mp'}, use_global_device_ids=true, to_apply=%region_9.10 | all-reduce | flops 2 | bytes 16 | tf_op jit(solution)/shard_map/psum | solution.py:73
  317.9 5.9 %bitcast_convert_fusion = bf16[512,1024]{1,0:T(8,128)(2,1)} fusion(bf16[4,512,512]{1,2,0:T(8,128)(2,1)} %all-gather.3.cloned.1.call-done, bf16[3,512,1024]{2,1,0:T(8,128)(2,1)} %copy-done.1, bf16[1,512,1024]{2,1,0:T(8,128)(2,1)S(1)} %bitcast.51), kind=kOutput, calls=%fused_computation.13 | convolution fusion | flops 2150105088 | bytes 7340032 | tf_op jit(solution)/shard_map/kij,kjd->id/dot_general | solution.py:74
  323.7 3.9 %add_convert_fusion = bf16[512,1024]{1,0:T(8,128)(2,1)} fusion(bf16[512,1024]{1,0:T(8,128)(2,1)} %collective-permute-done.8, bf16[512,1024]{1,0:T(8,128)(2,1)} %collective-permute-done.7, bf16[512,1024]{1,0:T(8,128)(2,1)} %collective-permute-done.6, bf16[512,1024]{1,0:T(8,128)(2,1)S(1)} %copy-done, bf16[4,512,512]{1,2,0:T(8,128)(2,1)} %all-gather.5.cloned.1.call-done), kind=kOutput, calls=%fused_computation.14 | convolution fusion | flops 540540928 | bytes 5767168 | tf_op jit(solution)/shard_map/ij,id->jd/dot_general | solution.py:77
  (43 shorter events, 4.6 us)
Async XLA Ops:
  7.2 84.6 %copy-start = (bf16[512,1024]{1,0:T(8,128)(2,1)S(1)}, bf16[512,1024]{1,0:T(8,128)(2,1)}, u32[]{:S(2)}) copy-start(bf16[512,1024]{1,0:T(8,128)(2,1)} %param.7) | copy-start | bytes 3145732
  7.2 157.7 %reduce-scatter.2.cloned.1.call-start = ((), (), s32[]{:S(2)}) async-start(), calls=%async_computation.1 | async-start | bytes 5242880 | tf_op jit(solution)/shard_map/reduce_scatter | solution.py:47
  7.2 29.0 %collective-permute-start.2 = (bf16[512,1024]{1,0:T(8,128)(2,1)}, bf16[512,1024]{1,0:T(8,128)(2,1)S(1)}, u32[]{:S(2)}, u32[]{:S(2)}) collective-permute-start(bf16[512,1024]{1,0:T(8,128)(2,1)} %param.8), channel_id=1, source_target_pairs={{0,20},{4,24},{8,28},{12,0},{16,4},{20,8},{24,12},{28,16},{1,21},{... | collective-permute-start | bytes 3145736 | tf_op jit(solution)/shard_map/ppermute | solution.py:14
  12.3 47.6 %collective-permute-start.1 = (bf16[512,1024]{1,0:T(8,128)(2,1)}, bf16[512,1024]{1,0:T(8,128)(2,1)S(1)}, u32[]{:S(2)}, u32[]{:S(2)}) collective-permute-start(bf16[512,1024]{1,0:T(8,128)(2,1)} %param.8), channel_id=1, source_target_pairs={{0,24},{4,28},{8,0},{12,4},{16,8},{20,12},{24,16},{28,20},{1,25},{... | collective-permute-start | bytes 3145736 | tf_op jit(solution)/shard_map/ppermute | solution.py:14
  13.6 66.4 %collective-permute-start = (bf16[512,1024]{1,0:T(8,128)(2,1)}, bf16[512,1024]{1,0:T(8,128)(2,1)}, u32[]{:S(2)}, u32[]{:S(2)}) collective-permute-start(bf16[512,1024]{1,0:T(8,128)(2,1)} %param.8), channel_id=1, source_target_pairs={{0,28},{4,0},{8,4},{12,8},{16,12},{20,16},{24,20},{28,24},{1,29},{... | collective-permute-start | bytes 3145736 | tf_op jit(solution)/shard_map/ppermute | solution.py:14
  87.7 4.0 %copy-start.5 = (bf16[512,1024]{1,0:T(8,128)(2,1)S(1)}, bf16[512,1024]{1,0:T(8,128)(2,1)}, u32[]{:S(2)}) copy-start(bf16[512,1024]{1,0:T(8,128)(2,1)} %param.8) | copy-start | bytes 3145732
  90.0 1.7 copy-start.1
  96.0 0.7 copy-start.3
  96.0 29.1 %copy-start.2 = (s32[1,3]{1,0:T(1,128)S(1)}, s32[1,3]{1,0:T(1,128)}, u32[]{:S(2)}) copy-start(s32[1,3]{1,0:T(1,128)} %param.11) | copy-start | bytes 40
  96.0 29.2 %copy-start.4 = (bf16[512]{0:T(512)(128)(2,1)S(1)}, bf16[512]{0:T(512)(128)(2,1)}, u32[]{:S(2)}) copy-start(bf16[512]{0:T(512)(128)(2,1)} %param.9) | copy-start | bytes 3076
  96.1 97.1 %all-gather.5.cloned.1.call-start = ((), (), s32[]{:S(2)}) async-start(), calls=%async_computation.3 | async-start | bytes 2621440 | tf_op jit(solution)/shard_map/all_gather | solution.py:71
  96.7 28.7 %collective-permute-start.5 = (bf16[512]{0:T(512)(128)(2,1)S(1)}, bf16[512]{0:T(512)(128)(2,1)S(1)}, u32[]{:S(2)}, u32[]{:S(2)}) collective-permute-start(bf16[512]{0:T(512)(128)(2,1)S(1)} %copy-done.3), channel_id=1, source_target_pairs={{0,20},{4,24},{8,28},{12,0},{16,4},{20,8},{24,12},{28,16},{1,21},{... | collective-permute-start | bytes 3080 | tf_op jit(solution)/shard_map/ppermute | solution.py:14
  100.0 26.4 %collective-permute-start.4 = (bf16[512]{0:T(512)(128)(2,1)S(1)}, bf16[512]{0:T(512)(128)(2,1)S(1)}, u32[]{:S(2)}, u32[]{:S(2)}) collective-permute-start(bf16[512]{0:T(512)(128)(2,1)S(1)} %copy-done.3), channel_id=1, source_target_pairs={{0,24},{4,28},{8,0},{12,4},{16,8},{20,12},{24,16},{28,20},{1,25},{... | collective-permute-start | bytes 3080 | tf_op jit(solution)/shard_map/ppermute | solution.py:14
  123.8 3.6 %collective-permute-start.3 = (bf16[512]{0:T(512)(128)(2,1)S(1)}, bf16[512]{0:T(512)(128)(2,1)S(1)}, u32[]{:S(2)}, u32[]{:S(2)}) collective-permute-start(bf16[512]{0:T(512)(128)(2,1)S(1)} %copy-done.3), channel_id=1, source_target_pairs={{0,28},{4,0},{8,4},{12,8},{16,12},{20,16},{24,20},{28,24},{1,29},{... | collective-permute-start | bytes 3080 | tf_op jit(solution)/shard_map/ppermute | solution.py:14
  170.2 147.7 %all-gather.3.cloned.1.call-start = ((), (), s32[]{:S(2)}) async-start(), calls=%async_computation.2 | async-start | bytes 2621440 | tf_op jit(solution)/shard_map/all_gather | solution.py:70
  198.6 125.1 %collective-permute-start.8 = (bf16[512,1024]{1,0:T(8,128)(2,1)}, bf16[512,1024]{1,0:T(8,128)(2,1)}, u32[]{:S(2)}, u32[]{:S(2)}) collective-permute-start(bf16[512,1024]{1,0:T(8,128)(2,1)} %get-tuple-element.4), channel_id=1, source_target_pairs={{0,12},{4,16},{8,20},{12,24},{16,28},{20,0},{24,4},{28,8},{1,13},{... | collective-permute-start | bytes 3145736 | tf_op jit(solution)/shard_map/ppermute | solution.py:14
  201.0 122.7 %collective-permute-start.7 = (bf16[512,1024]{1,0:T(8,128)(2,1)}, bf16[512,1024]{1,0:T(8,128)(2,1)}, u32[]{:S(2)}, u32[]{:S(2)}) collective-permute-start(bf16[512,1024]{1,0:T(8,128)(2,1)} %get-tuple-element.5), channel_id=1, source_target_pairs={{0,8},{4,12},{8,16},{12,20},{16,24},{20,28},{24,0},{28,4},{1,9},{5... | collective-permute-start | bytes 3145736 | tf_op jit(solution)/shard_map/ppermute | solution.py:14
  202.5 121.2 %collective-permute-start.6 = (bf16[512,1024]{1,0:T(8,128)(2,1)S(1)}, bf16[512,1024]{1,0:T(8,128)(2,1)}, u32[]{:S(2)}, u32[]{:S(2)}) collective-permute-start(bf16[512,1024]{1,0:T(8,128)(2,1)S(1)} %get-tuple-element.3), channel_id=1, source_target_pairs={{0,4},{4,8},{8,12},{12,16},{16,20},{20,24},{24,28},{28,0},{1,5},{5... | collective-permute-start | bytes 3145736 | tf_op jit(solution)/shard_map/ppermute | solution.py:14
Sparse Core Ops, SparseCore 0:
  96.2 68.6 reduce-scatter.1
  170.3 22.7 all-gather.4
  195.3 23.1 all-gather.2
where the time goes:
time: 336 us; the launch traced here: 335 us
  waiting for transfers between devices  122 us (36%)
  blocking collectives  112 us (33%)
  starting transfers between devices  40.1 us (12%)
  matrix products  19.5 us (6%)
  other arithmetic  16.7 us (5%)
  between operations  16.3 us (5%)
  local copies, waits for them, and re-layouts  8.01 us (2%)
    psum x1, blocking collectives, local(): loss_all, valid_all = lax.psum((loss_sum, valid_sum), ('dp', 'mp'))  112 us
    ppermute x9, waiting for transfers between devices, shifted(): return lax.ppermute(value, axis, pairs)  62.3 us
    ppermute x9, starting transfers between devices, shifted(): return lax.ppermute(value, axis, pairs)  40 us
    reduce_scatter x1, waiting for transfers between devices, local(): summed = lax.psum_scatter(raw, 'mp', scatter_dimension=1, tiled=True)  36.8 us
    all_gather x1, waiting for transfers between devices, local(): lax.all_gather(row_weight, 'mp', axis=1, tiled=True)  22.2 us
  transfers between devices with their start and end apart: 12, of which 7 were waited for; matrix products, arithmetic and copies ran while one was open for 5% of the time, Pallas kernels for 0%

commit v1 on v0

--- a/solution.py
+++ b/solution.py
@@ -3,6 +3,7 @@
 import jax.numpy as jnp
 from jax import lax
 from jax.sharding import PartitionSpec as P
+from jax.lax import psum
 
 D = 4096
 WIN = 3
@@ -70,7 +71,7 @@
         lax.all_gather(key_weight, "mp", axis=1, tiled=True),
         lax.all_gather(row_weight, "mp", axis=1, tiled=True),
     )
-    loss_all, valid_all = lax.psum((loss_sum, valid_sum), ("dp", "mp"))
+    loss_all, valid_all = psum(psum((loss_sum, valid_sum), "mp"), axis_name="dp")
     grad_query = jnp.einsum(
         "kij,kjd->id", key_weight, keys, preferred_element_type=jnp.float32
     ).astype(jnp.bfloat16)

time: 336 us -> 320 us (0.952); the launches traced: 335 us -> 315 us
  blocking collectives: 112 us -> 91.8 us
    psum x1 -> x2, blocking collectives: 112 us -> 91.8 us  [the longest x1 84.7 us: local(): psum(psum((loss_sum, valid_sum), 'mp'), axis_name='dp')]
  transfers between devices with their start and end apart: 12 -> 12, of which waited for: 7 -> 7; matrix products, arithmetic and copies ran while one was open for 5% -> 6% of each run, Pallas kernels for 0% -> 0%
where the time goes in v1:
time: 320 us; the launch traced here: 315 us
  waiting for transfers between devices  122 us (38%)
  blocking collectives  91.8 us (29%)
  starting transfers between devices  40.1 us (13%)
  matrix products  19.5 us (6%)
  other arithmetic  16.7 us (5%)
  between operations  16.3 us (5%)
  local copies, waits for them, and re-layouts  8.01 us (3%)
    psum x1, blocking collectives, local(): psum(psum((loss_sum, valid_sum), 'mp'), axis_name='dp')  84.7 us
    ppermute x9, waiting for transfers between devices, shifted(): return lax.ppermute(value, axis, pairs)  62.3 us
    ppermute x9, starting transfers between devices, shifted(): return lax.ppermute(value, axis, pairs)  40 us
    reduce_scatter x1, waiting for transfers between devices, local(): summed = lax.psum_scatter(raw, 'mp', scatter_dimension=1, tiled=True)  36.8 us
    all_gather x1, waiting for transfers between devices, local(): lax.all_gather(row_weight, 'mp', axis=1, tiled=True)  22.2 us
    psum x1, blocking collectives, local(): psum((loss_sum, valid_sum), 'mp')  7.17 us
  transfers between devices with their start and end apart: 12, of which 7 were waited for; matrix products, arithmetic and copies ran while one was open for 6% of the time, Pallas kernels for 0%

profile of v1, /device:TPU:0, one launch (start us, length us, event | category | flops | bytes accessed | tf_op | source)
XLA Modules:
  0.0 314.6 jit_solution(11171668952502765720)
XLA Ops:
  7.2 5.1 %collective-permute-start.2 = (bf16[512,1024]{1,0:T(8,128)(2,1)}, bf16[512,1024]{1,0:T(8,128)(2,1)S(1)}, u32[]{:S(2)}, u32[]{:S(2)}) collective-permute-start(bf16[512,1024]{1,0:T(8,128)(2,1)} %param.8), channel_id=1, source_target_pairs={{0,20},{4,24},{8,28},{12,0},{16,4},{20,8},{24,12},{28,16},{1,21},{... | collective-permute-start | bytes 3145736 | tf_op jit(solution)/shard_map/ppermute | solution.py:15
  12.3 1.3 collective-permute-start.1
  14.2 1.4 fusion.12
  15.6 2.1 pad_add_fusion.1
  18.9 0.7 broadcast_select_fusion.2
  19.6 16.6 %collective-permute-done.2 = bf16[512,1024]{1,0:T(8,128)(2,1)S(1)} collective-permute-done((bf16[512,1024]{1,0:T(8,128)(2,1)}, bf16[512,1024]{1,0:T(8,128)(2,1)S(1)}, u32[]{:S(2)}, u32[]{:S(2)}) %collective-permute-start.2) | collective-permute-done | bytes 1048608 | tf_op jit(solution)/shard_map/ppermute | solution.py:15
  36.2 23.7 %collective-permute-done.1 = bf16[512,1024]{1,0:T(8,128)(2,1)S(1)} collective-permute-done((bf16[512,1024]{1,0:T(8,128)(2,1)}, bf16[512,1024]{1,0:T(8,128)(2,1)S(1)}, u32[]{:S(2)}, u32[]{:S(2)}) %collective-permute-start.1) | collective-permute-done | bytes 1048608 | tf_op jit(solution)/shard_map/ppermute | solution.py:15
  59.9 20.1 %collective-permute-done = bf16[512,1024]{1,0:T(8,128)(2,1)} collective-permute-done((bf16[512,1024]{1,0:T(8,128)(2,1)}, bf16[512,1024]{1,0:T(8,128)(2,1)}, u32[]{:S(2)}, u32[]{:S(2)}) %collective-permute-start) | collective-permute-done | bytes 1048608 | tf_op jit(solution)/shard_map/ppermute | solution.py:15
  80.0 3.2 %pad_maximum_fusion.1 = bf16[3,512,1024]{2,1,0:T(8,128)(2,1)} fusion(bf16[1,512,1024]{2,1,0:T(8,128)(2,1)S(1)} %bitcast.48, bf16[1,512,1024]{2,1,0:T(8,128)(2,1)S(1)} %bitcast.49, bf16[1,512,1024]{2,1,0:T(8,128)(2,1)} %bitcast.9), kind=kLoop, calls=%fused_computation.4 | loop fusion | flops 3145728 | bytes 6291456 | tf_op jit(solution)/shard_map/stack | solution.py:38
  83.2 4.4 %gather_fusion.1 = bf16[3,512,1024]{2,1,0:T(8,128)(2,1)} fusion(bf16[3,512,1024]{2,1,0:T(8,128)(2,1)} %pad_maximum_fusion.1, s32[1024]{0:T(1024)S(1)} %pad_clamp_fusion), kind=kCustom, calls=%fused_computation.1 | custom fusion | bytes 6291468 | tf_op jit(solution)/shard_map/jit(_take)/gather | solution.py:38
  87.7 2.3 broadcast_select_fusion
  90.0 1.7 copy-done.1
  91.7 4.3 %fusion.2 = f32[4,512,512]{1,2,0:T(8,128)} fusion(bf16[3,512,1024]{2,1,0:T(8,128)(2,1)S(1)} %broadcast_select_fusion, bf16[1,512,1024]{2,1,0:T(8,128)(2,1)S(1)} %bitcast.50, bf16[512,1024]{1,0:T(8,128)(2,1)S(1)} %copy-done), kind=kOutput, calls=%fused_computation.12 | convolution fusion | flops 2149580800 | bytes 9437184 | tf_op jit(solution)/shard_map/id,kjd->kij/dot_general | solution.py:45
  96.7 3.3 %collective-permute-start.5 = (bf16[512]{0:T(512)(128)(2,1)S(1)}, bf16[512]{0:T(512)(128)(2,1)S(1)}, u32[]{:S(2)}, u32[]{:S(2)}) collective-permute-start(bf16[512]{0:T(512)(128)(2,1)S(1)} %copy-done.3), channel_id=1, source_target_pairs={{0,20},{4,24},{8,28},{12,0},{16,4},{20,8},{24,12},{28,16},{1,21},{... | collective-permute-start | bytes 3080 | tf_op jit(solution)/shard_map/ppermute | solution.py:15
  100.0 23.8 %collective-permute-start.4 = (bf16[512]{0:T(512)(128)(2,1)S(1)}, bf16[512]{0:T(512)(128)(2,1)S(1)}, u32[]{:S(2)}, u32[]{:S(2)}) collective-permute-start(bf16[512]{0:T(512)(128)(2,1)S(1)} %copy-done.3), channel_id=1, source_target_pairs={{0,24},{4,28},{8,0},{12,4},{16,8},{20,12},{24,16},{28,20},{1,25},{... | collective-permute-start | bytes 3080 | tf_op jit(solution)/shard_map/ppermute | solution.py:15
  124.5 0.7 pad_add_fusion.2
  125.5 0.9 collective-permute-done.4
  126.4 1.0 collective-permute-done.3
  128.1 36.8 %reduce-scatter.2.cloned.1.call-done = f32[4,128,512]{1,2,0:T(8,128)} async-done(((f32[4,512,512]{1,2,0:T(8,128)}), f32[4,128,512]{1,2,0:T(8,128)}) %reduce-scatter.2.cloned.1.call-update) | async-done | bytes 1048592 | tf_op jit(solution)/shard_map/reduce_scatter | solution.py:48
  164.8 1.8 select_reduce_fusion.3
  167.6 1.3 convert_reduce_fusion
  168.9 1.3 multiply_convert_fusion
  170.3 0.7 all-gather.3.cloned.1.call-update
  170.9 22.2 %all-gather.5.cloned.1.call-done = bf16[4,512,512]{1,2,0:T(8,128)(2,1)} async-done(((bf16[4,128,512]{1,2,0:T(8,128)(2,1)}), bf16[4,512,512]{1,2,0:T(8,128)(2,1)}) %all-gather.5.cloned.1.call-update) | async-done | bytes 2097168 | tf_op jit(solution)/shard_map/all_gather | solution.py:72
  193.2 5.5 %select_reduce_fusion.2 = (bf16[512,1024]{1,0:T(8,128)(2,1)S(1)}, bf16[512,1024]{1,0:T(8,128)(2,1)}, bf16[512,1024]{1,0:T(8,128)(2,1)}) fusion(pred[3]{0:T(512)(128)(4,1)S(1)} %get-tuple-element.26, pred[3]{0:T(512)(128)(4,1)S(1)} %get-tuple-element.28, pred[3]{0:T(512)(128)(4,1)S(1)} %get-tuple-element.25, ...), kind=kOutput, calls=%fused_computation.7 | convolution fusion | flops 1620049920 | bytes 6291465 | tf_op jit(solution)/shard_map/kij,id->kjd/dot_general | solution.py:79
  198.6 2.4 collective-permute-start.8
  201.0 1.5 collective-permute-start.7
  202.5 1.5 collective-permute-start.6
  204.0 7.2 %all-reduce.1 = (f32[]{:T(128)}, f32[]{:T(128)}) all-reduce(f32[]{:T(128)} %get-tuple-element.7, f32[]{:T(128)} %get-tuple-element.6), channel_id=1, replica_groups=mesh['dp'=8,'mp'=4] {'mp'}, use_global_device_ids=true, to_apply=%region_9.10 | all-reduce | flops 2 | bytes 16 | tf_op jit(solution)/shard_map/psum | solution.py:74
  211.2 84.7 %all-reduce = (f32[]{:T(128)}, f32[]{:T(128)}) all-reduce(f32[]{:T(128)} %get-tuple-element.14, f32[]{:T(128)} %get-tuple-element.15), channel_id=1, replica_groups=mesh['dp'=8,'mp'=4] {'dp'}, use_global_device_ids=true, to_apply=%region_10.11 | all-reduce | flops 2 | bytes 16 | tf_op jit(solution)/shard_map/psum | solution.py:74
  297.1 5.9 %bitcast_convert_fusion = bf16[512,1024]{1,0:T(8,128)(2,1)} fusion(bf16[4,512,512]{1,2,0:T(8,128)(2,1)} %all-gather.3.cloned.1.call-done, bf16[3,512,1024]{2,1,0:T(8,128)(2,1)} %copy-done.1, bf16[1,512,1024]{2,1,0:T(8,128)(2,1)S(1)} %bitcast.51), kind=kOutput, calls=%fused_computation.13 | convolution fusion | flops 2150105088 | bytes 7340032 | tf_op jit(solution)/shard_map/kij,kjd->id/dot_general | solution.py:75
  303.0 3.9 %add_convert_fusion = bf16[512,1024]{1,0:T(8,128)(2,1)} fusion(bf16[512,1024]{1,0:T(8,128)(2,1)} %collective-permute-done.8, bf16[512,1024]{1,0:T(8,128)(2,1)} %collective-permute-done.7, bf16[512,1024]{1,0:T(8,128)(2,1)} %collective-permute-done.6, bf16[512,1024]{1,0:T(8,128)(2,1)S(1)} %copy-done, bf16[4,512,512]{1,2,0:T(8,128)(2,1)} %all-gather.5.cloned.1.call-done), kind=kOutput, calls=%fused_computation.14 | convolution fusion | flops 540540928 | bytes 5767168 | tf_op jit(solution)/shard_map/ij,id->jd/dot_general | solution.py:78
  (44 shorter events, 5.2 us)
Async XLA Ops:
  7.2 84.6 %copy-start = (bf16[512,1024]{1,0:T(8,128)(2,1)S(1)}, bf16[512,1024]{1,0:T(8,128)(2,1)}, u32[]{:S(2)}) copy-start(bf16[512,1024]{1,0:T(8,128)(2,1)} %param.7) | copy-start | bytes 3145732
  7.2 157.7 %reduce-scatter.2.cloned.1.call-start = ((), (), s32[]{:S(2)}) async-start(), calls=%async_computation.1 | async-start | bytes 5242880 | tf_op jit(solution)/shard_map/reduce_scatter | solution.py:48
  7.2 29.0 %collective-permute-start.2 = (bf16[512,1024]{1,0:T(8,128)(2,1)}, bf16[512,1024]{1,0:T(8,128)(2,1)S(1)}, u32[]{:S(2)}, u32[]{:S(2)}) collective-permute-start(bf16[512,1024]{1,0:T(8,128)(2,1)} %param.8), channel_id=1, source_target_pairs={{0,20},{4,24},{8,28},{12,0},{16,4},{20,8},{24,12},{28,16},{1,21},{... | collective-permute-start | bytes 3145736 | tf_op jit(solution)/shard_map/ppermute | solution.py:15
  12.3 47.6 %collective-permute-start.1 = (bf16[512,1024]{1,0:T(8,128)(2,1)}, bf16[512,1024]{1,0:T(8,128)(2,1)S(1)}, u32[]{:S(2)}, u32[]{:S(2)}) collective-permute-start(bf16[512,1024]{1,0:T(8,128)(2,1)} %param.8), channel_id=1, source_target_pairs={{0,24},{4,28},{8,0},{12,4},{16,8},{20,12},{24,16},{28,20},{1,25},{... | collective-permute-start | bytes 3145736 | tf_op jit(solution)/shard_map/ppermute | solution.py:15
  13.6 66.4 %collective-permute-start = (bf16[512,1024]{1,0:T(8,128)(2,1)}, bf16[512,1024]{1,0:T(8,128)(2,1)}, u32[]{:S(2)}, u32[]{:S(2)}) collective-permute-start(bf16[512,1024]{1,0:T(8,128)(2,1)} %param.8), channel_id=1, source_target_pairs={{0,28},{4,0},{8,4},{12,8},{16,12},{20,16},{24,20},{28,24},{1,29},{... | collective-permute-start | bytes 3145736 | tf_op jit(solution)/shard_map/ppermute | solution.py:15
  87.7 4.0 %copy-start.5 = (bf16[512,1024]{1,0:T(8,128)(2,1)S(1)}, bf16[512,1024]{1,0:T(8,128)(2,1)}, u32[]{:S(2)}) copy-start(bf16[512,1024]{1,0:T(8,128)(2,1)} %param.8) | copy-start | bytes 3145732
  90.0 1.7 copy-start.1
  96.0 0.7 copy-start.3
  96.0 29.1 %copy-start.2 = (s32[1,3]{1,0:T(1,128)S(1)}, s32[1,3]{1,0:T(1,128)}, u32[]{:S(2)}) copy-start(s32[1,3]{1,0:T(1,128)} %param.11) | copy-start | bytes 40
  96.0 29.2 %copy-start.4 = (bf16[512]{0:T(512)(128)(2,1)S(1)}, bf16[512]{0:T(512)(128)(2,1)}, u32[]{:S(2)}) copy-start(bf16[512]{0:T(512)(128)(2,1)} %param.9) | copy-start | bytes 3076
  96.1 97.1 %all-gather.5.cloned.1.call-start = ((), (), s32[]{:S(2)}) async-start(), calls=%async_computation.3 | async-start | bytes 2621440 | tf_op jit(solution)/shard_map/all_gather | solution.py:72
  96.7 28.7 %collective-permute-start.5 = (bf16[512]{0:T(512)(128)(2,1)S(1)}, bf16[512]{0:T(512)(128)(2,1)S(1)}, u32[]{:S(2)}, u32[]{:S(2)}) collective-permute-start(bf16[512]{0:T(512)(128)(2,1)S(1)} %copy-done.3), channel_id=1, source_target_pairs={{0,20},{4,24},{8,28},{12,0},{16,4},{20,8},{24,12},{28,16},{1,21},{... | collective-permute-start | bytes 3080 | tf_op jit(solution)/shard_map/ppermute | solution.py:15
  100.0 26.4 %collective-permute-start.4 = (bf16[512]{0:T(512)(128)(2,1)S(1)}, bf16[512]{0:T(512)(128)(2,1)S(1)}, u32[]{:S(2)}, u32[]{:S(2)}) collective-permute-start(bf16[512]{0:T(512)(128)(2,1)S(1)} %copy-done.3), channel_id=1, source_target_pairs={{0,24},{4,28},{8,0},{12,4},{16,8},{20,12},{24,16},{28,20},{1,25},{... | collective-permute-start | bytes 3080 | tf_op jit(solution)/shard_map/ppermute | solution.py:15
  123.8 3.6 %collective-permute-start.3 = (bf16[512]{0:T(512)(128)(2,1)S(1)}, bf16[512]{0:T(512)(128)(2,1)S(1)}, u32[]{:S(2)}, u32[]{:S(2)}) collective-permute-start(bf16[512]{0:T(512)(128)(2,1)S(1)} %copy-done.3), channel_id=1, source_target_pairs={{0,28},{4,0},{8,4},{12,8},{16,12},{20,16},{24,20},{28,24},{1,29},{... | collective-permute-start | bytes 3080 | tf_op jit(solution)/shard_map/ppermute | solution.py:15
  170.2 126.9 %all-gather.3.cloned.1.call-start = ((), (), s32[]{:S(2)}) async-start(), calls=%async_computation.2 | async-start | bytes 2621440 | tf_op jit(solution)/shard_map/all_gather | solution.py:71
  198.6 104.4 %collective-permute-start.8 = (bf16[512,1024]{1,0:T(8,128)(2,1)}, bf16[512,1024]{1,0:T(8,128)(2,1)}, u32[]{:S(2)}, u32[]{:S(2)}) collective-permute-start(bf16[512,1024]{1,0:T(8,128)(2,1)} %get-tuple-element.4), channel_id=1, source_target_pairs={{0,12},{4,16},{8,20},{12,24},{16,28},{20,0},{24,4},{28,8},{1,13},{... | collective-permute-start | bytes 3145736 | tf_op jit(solution)/shard_map/ppermute | solution.py:15
  201.0 102.0 %collective-permute-start.7 = (bf16[512,1024]{1,0:T(8,128)(2,1)}, bf16[512,1024]{1,0:T(8,128)(2,1)}, u32[]{:S(2)}, u32[]{:S(2)}) collective-permute-start(bf16[512,1024]{1,0:T(8,128)(2,1)} %get-tuple-element.5), channel_id=1, source_target_pairs={{0,8},{4,12},{8,16},{12,20},{16,24},{20,28},{24,0},{28,4},{1,9},{5... | collective-permute-start | bytes 3145736 | tf_op jit(solution)/shard_map/ppermute | solution.py:15
  202.5 100.5 %collective-permute-start.6 = (bf16[512,1024]{1,0:T(8,128)(2,1)S(1)}, bf16[512,1024]{1,0:T(8,128)(2,1)}, u32[]{:S(2)}, u32[]{:S(2)}) collective-permute-start(bf16[512,1024]{1,0:T(8,128)(2,1)S(1)} %get-tuple-element.3), channel_id=1, source_target_pairs={{0,4},{4,8},{8,12},{12,16},{16,20},{20,24},{24,28},{28,0},{1,5},{5... | collective-permute-start | bytes 3145736 | tf_op jit(solution)/shard_map/ppermute | solution.py:15
Sparse Core Ops, SparseCore 0:
  96.2 68.6 reduce-scatter.1
  170.3 22.8 all-gather.4
  195.3 22.9 all-gather.2
